TPU v7x, 32 devices: a whole 2x2x4 slice. The times are simulated.
32 devices in a mesh: pre: 2 (over y), dec: 4 (over x, core), rep: 4 (over z).
Axes of the slice: x: 2, y: 2, z: 4, core: 2. Of those that a mesh axis runs over, the one named last changes fastest.
Arguments:
- layer_queries: bfloat16 [2048, 8192], P(('pre', 'rep'), 'dec'), may hold values from -16 to 16
- layer_keys: bfloat16 [2048, 1024], P(('pre', 'rep')), may hold values from -16 to 16
- layer_values: bfloat16 [2048, 1024], P(('pre', 'rep')), may hold values from -6 to 6
- query_bias: float32 [8192], P('dec'), may hold values from -3 to 3
- key_bias: float32 [1024], replicated, may hold values from -3 to 3
- value_bias: float32 [1024], replicated, may hold values from -3 to 3
- positions: int32 [2048], replicated, may hold values from 0 to 2047, each once
- lengths: int32 [32], replicated, may hold values from 1 to 1024, as said below
- replica_of: int32 [32], replicated, may hold values from 0 to 3, as said below
- page_table: int32 [4, 16], replicated, may hold values from 0 to 3, as said below
- prefill_cache: bfloat16 [4, 16, 16, 4, 64, 128], P('rep', 'pre', 'dec'), may hold values from -6 to 6
Outputs:
- context: bfloat16 [2048, 8192], P(('pre', 'rep'), 'dec')
- decode_cache: bfloat16 [4, 4, 8, 16, 4, 64, 128], P('rep', 'dec', None, 'pre')
Inputs may be any that keep to these rules, and one draw needn't show every extreme that they name: `replica_of`: each replica receives exactly 8 requests. `lengths`: the requests of each replica fill exactly 16 blocks of 128 tokens, each request starting a new block; in each replica one request spans exactly 8 full blocks. `page_table`: in each aligned run of 8 blocks of a replica, exactly half of the 4 decode devices appear, each exactly 4 times.
All inputs are finite; a program needn't handle non-finite values.
Results may differ from a plain program's by a relative error of at most 0.0094.
Values may be sent and summed in bfloat16 or wider, within the bound.
No kernel may reach another device: no remote copies, remote signals or barrier semaphores. Data moves between devices by JAX's collectives and lax.ppermute only.
A program may use at most 128 MiB of HBM per device.

v0:
```python
import jax
import jax.numpy as jnp
from jax import lax
from jax.sharding import PartitionSpec as P

HEADS = 64
KVH = 8
HD = 128
BLOCK = 128
rope_base = 1000000.0
masked_score = -1e30


def rotate(values, where_at):
    width = values.shape[-1]
    half_width = width // 2
    freqs = 1.0 / rope_base ** (jnp.arange(half_width, dtype=jnp.float32) * (2.0 / width))
    angles = where_at.astype(jnp.float32)[:, None] * freqs[None, :]
    cosine = jnp.cos(angles)[:, None, :]
    sine = jnp.sin(angles)[:, None, :]
    first = values[..., :half_width]
    second = values[..., half_width:]
    return jnp.concatenate(
        [first * cosine - second * sine, second * cosine + first * sine], axis=-1
    )


def valid_tokens(lengths, replica_of, replica, block_ids):
    member = replica_of == replica
    counts = jnp.where(member, (lengths + (BLOCK - 1)) // BLOCK, 0)
    starts = jnp.cumsum(counts) - counts
    inside = (block_ids[:, None] >= starts[None, :]) & (
        block_ids[:, None] < (starts + counts)[None, :]
    )
    remain = lengths[None, :] - BLOCK * (block_ids[:, None] - starts[None, :])
    return jnp.sum(jnp.where(inside, jnp.clip(remain, 0, BLOCK), 0), axis=1)


def shards(
    layer_queries,
    layer_keys,
    layer_values,
    query_bias,
    key_bias,
    value_bias,
    positions,
    lengths,
    replica_of,
    page_table,
    prefill_cache,
):
    row_count = layer_queries.shape[0]
    head_count = layer_queries.shape[1] // HD
    group_size = HEADS // KVH
    kv_local = max(1, head_count // group_size)
    per_group = head_count // kv_local
    scale = HD ** (-0.5)
    row_start = lax.axis_index(("pre", "rep")) * row_count
    query_pos = lax.dynamic_slice_in_dim(positions, row_start, row_count)
    shifted = layer_queries.astype(jnp.float32).reshape(
        row_count, head_count, HD
    ) + query_bias.reshape(head_count, HD)
    rotated = rotate(shifted, query_pos).astype(jnp.bfloat16)
    query_rows = (
        rotated.reshape(row_count, kv_local, per_group, HD)
        .transpose(1, 2, 0, 3)
        .reshape(kv_local, per_group * row_count, HD)
    )
    query_rowpos = jnp.tile(query_pos, per_group)
    kv_first = lax.axis_index("dec") * head_count // group_size
    bias_keys = lax.dynamic_slice_in_dim(key_bias, kv_first * HD, kv_local * HD).reshape(
        kv_local, HD
    )
    bias_values = lax.dynamic_slice_in_dim(value_bias, kv_first * HD, kv_local * HD).reshape(
        kv_local, HD
    )
    own_keys = lax.dynamic_slice_in_dim(layer_keys, kv_first * HD, kv_local * HD, 1)
    own_values = lax.dynamic_slice_in_dim(layer_values, kv_first * HD, kv_local * HD, 1)
    count = own_keys.shape[0]
    shifted_keys = own_keys.astype(jnp.float32).reshape(count, kv_local, HD) + bias_keys
    keys_rot = rotate(shifted_keys, query_pos).astype(jnp.bfloat16).reshape(count, kv_local * HD)
    values_biased = (
        own_values.astype(jnp.float32).reshape(count, kv_local, HD) + bias_values
    ).astype(jnp.bfloat16)
    local_values = values_biased.reshape(count, kv_local * HD)
    best = jnp.full((kv_local, per_group * row_count), masked_score, jnp.float32)
    piece_keys = lax.all_gather(keys_rot, ("pre", "rep"), axis=0, tiled=True)
    piece_values = lax.all_gather(local_values, ("pre", "rep"), axis=0, tiled=True)
    count = piece_keys.shape[0]
    scores = (
        jnp.einsum(
            "kqd,nkd->kqn",
            query_rows,
            piece_keys.reshape(count, kv_local, HD),
            preferred_element_type=jnp.float32,
        )
        * scale
    )
    allowed = positions[None, None, :] <= query_rowpos[None, :, None]
    scores = jnp.where(allowed, scores, masked_score)
    newest = jnp.maximum(best, jnp.max(scores, axis=2))
    weights = jnp.where(allowed, jnp.exp(scores - newest[:, :, None]), 0.0)
    total = jnp.sum(weights, axis=2)
    added = jnp.einsum(
        "kqn,nkd->kqd",
        weights.astype(jnp.bfloat16),
        piece_values.reshape(count, kv_local, HD),
        preferred_element_type=jnp.float32,
    )
    summed = added
    best, total, summed = (newest, total, summed)
    context = (summed / total[:, :, None]).astype(jnp.bfloat16)
    context = (
        context.reshape(kv_local, per_group, row_count, HD)
        .transpose(2, 0, 1, 3)
        .reshape(row_count, head_count * HD)
    )
    local_cache = prefill_cache[0]
    blk_count = local_cache.shape[0]
    dec_size = lax.axis_size("dec")
    pre_size = lax.axis_size("pre")
    capacity = 2 * blk_count // dec_size
    replica = lax.axis_index("rep")
    run_index = lax.axis_index("pre")
    block_ids = run_index * blk_count + jnp.arange(blk_count, dtype=jnp.int32)
    valid = valid_tokens(lengths, replica_of, replica, block_ids)
    keep = (jnp.arange(BLOCK, dtype=jnp.int32)[None, :] < valid[:, None]).astype(jnp.bfloat16)
    masked = local_cache * keep[:, None, None, None, :]
    page_row = lax.dynamic_index_in_dim(page_table, replica, 0, keepdims=False)
    targets = lax.dynamic_slice_in_dim(page_row, run_index * blk_count, blk_count)
    places = jnp.arange(blk_count, dtype=jnp.int32)
    before_me = (targets[None, :] == targets[:, None]) & (places[None, :] < places[:, None])
    ranks = jnp.sum(before_me, axis=1)
    select = (targets[None, None, :] == jnp.arange(dec_size, dtype=jnp.int32)[:, None, None]) & (
        ranks[None, None, :] == jnp.arange(capacity, dtype=jnp.int32)[None, :, None]
    )
    outgoing = jnp.dot(
        select.reshape(dec_size * capacity, blk_count).astype(jnp.bfloat16),
        masked.reshape(blk_count, -1),
        preferred_element_type=jnp.float32,
    ).astype(jnp.bfloat16)
    outgoing = outgoing.reshape((dec_size, capacity) + local_cache.shape[1:])
    group_halves = 2 * KVH // pre_size
    arrived = lax.all_to_all(
        lax.all_to_all(outgoing, "dec", split_axis=0, concat_axis=2, tiled=True),
        "pre",
        split_axis=2,
        concat_axis=0,
        tiled=True,
    )
    decode_cache = arrived.reshape(
        (1, 1, pre_size * capacity, group_halves) + local_cache.shape[2:]
    )
    return (context, decode_cache)


def solution(mesh):
    placed = (
        P(("pre", "rep"), "dec"),
        P(("pre", "rep"), None),
        P(("pre", "rep"), None),
        P("dec"),
        P(),
        P(),
        P(),
        P(),
        P(),
        P(),
        P("rep", "pre", "dec", None, None, None),
    )
    return jax.shard_map(
        shards,
        mesh=mesh,
        in_specs=placed,
        out_specs=(P(("pre", "rep"), "dec"), P("rep", "dec", None, "pre", None, None, None)),
        check_vma=False,
    )
```

profile of v0, /device:TPU:0, one launch (start us, length us, event | category | flops | bytes accessed | tf_op | source)
XLA Modules:
  0.0 157.9 jit_solution(5007270544340099804)
XLA Ops:
  7.2 0.0 copy-start
  7.2 0.0 all-gather.3.cloned.1.call-start
  7.3 1.0 dynamic-slice_convert_fusion
  8.3 0.1 copy.76
  8.4 0.8 dynamic-slice_bitcast_fusion
  9.2 0.1 broadcast_add_fusion
  9.3 0.8 fusion.14
  10.0 0.3 multiply_cosine_fusion
  10.4 0.7 pad_maximum_fusion.1
  11.1 0.0 all-gather.3.cloned.1.call-update
  11.1 0.7 compare_select_fusion
  11.8 0.1 copy.68
  11.9 0.1 reduce-window.8
  11.9 0.1 reduce
  12.0 0.8 select_reduce_fusion
  12.9 0.1 fusion.10
  13.0 3.0 %broadcast_multiply_fusion = bf16[1,8,4,4,64,128]{5,4,3,2,1,0:T(8,128)(2,1)} fusion(bf16[1,8,4,4,64,128]{5,4,3,2,1,0:T(8,128)(2,1)} %param.21, bf16[8,128]{1,0:T(8,128)(2,1)S(1)} %fusion.10), kind=kLoop, calls=%fused_computation.17 | loop fusion | flops 1048576 | bytes 4196352 | tf_op jit(solution)/shard_map/mul | solution.py:128
  16.0 2.5 %mul.158 = bf16[8,131072]{1,0:T(8,128)(2,1)S(1)} reshape(bf16[1,8,4,4,64,128]{5,4,3,2,1,0:T(8,128)(2,1)} %broadcast_multiply_fusion) | data formatting | bytes 4194304 | tf_op jit(solution)/shard_map/mul | solution.py:128
  18.5 0.8 dynamic-slice_bitcast_fusion.1
  19.3 0.2 convert_reduce_fusion
  19.5 1.2 fusion.6
  20.7 2.7 %copy.81 = bf16[2,8,1024,128]{3,2,1,0:T(8,128)(2,1)} copy(bf16[2,8,1024,128]{3,1,2,0:T(8,128)(2,1)S(1)} %fusion.6) | data formatting | bytes 8388608
  23.4 0.0 copy-start.3
  23.4 5.0 %all-to-all-start = ((bf16[4,4,4,4,64,128]{5,4,3,2,1,0:T(8,128)(2,1)}), bf16[4,4,4,4,64,128]{5,4,3,2,1,0:T(8,128)(2,1)}, u32[]{:S(2)}, u32[]{:S(2)}) async-start(bf16[4,4,4,4,64,128]{5,4,3,2,1,0:T(8,128)(2,1)} %bitcast.51), calls=%async_computation | async-start | bytes 8388608 | tf_op jit(solution)/shard_map/all_to_all | solution.py:145
  28.4 0.2 all-gather.5.cloned.1.call-start
  28.6 0.0 copy-done
  28.7 0.0 copy-start.5
  28.7 0.1 copy.77
  28.8 0.8 dynamic_slice.24
  29.6 0.8 add_convert_fusion.1
  30.3 0.0 all-gather.5.cloned.1.call-update
  30.3 0.1 copy.58
  30.4 0.1 copy.59
  30.5 0.0 copy-done.3
  30.6 0.2 convert_bitcast_fusion
  30.8 0.4 copy.79
  31.2 0.0 copy-done.5
  31.2 0.1 bitcast_add_fusion
  31.4 0.0 copy-start.4
  31.4 0.8 subtract_convert_fusion
  32.1 0.3 copy.60
  32.4 0.3 copy.61
  32.7 0.0 copy-done.4
  32.7 4.1 %broadcast_compare_fusion = pred[2048,2048]{0,1:T(8,128)(4,1)} fusion(s32[2048]{0:T(1024)S(1)} %bitcast.63, s32[2048]{0:T(1024)S(1)} %copy-done.4), kind=kLoop, calls=%fused_computation.8 | loop fusion | flops 4194304 | bytes 4210688 | tf_op jit(solution)/shard_map/le | solution.py:99
  36.9 1.6 pad_maximum_fusion
  38.4 15.1 %all-gather.3.cloned.1.call-done = bf16[2048,256]{0,1:T(8,128)(2,1)} async-done(((bf16[256,256]{0,1:T(8,128)(2,1)}), bf16[2048,256]{0,1:T(8,128)(2,1)}) %all-gather.3.cloned.1.call-update) | async-done | bytes 1048592 | tf_op jit(solution)/shard_map/all_gather | solution.py:87
  53.5 0.0 copy-start.2
  53.5 16.9 %fusion = (f32[2,2048]{1,0:T(2,128)S(1)}, f32[2,2048,2048]{1,2,0:T(8,128)}) fusion(pred[2048,2048]{0,1:T(8,128)(4,1)} %broadcast_compare_fusion, bf16[2,2048,128]{2,1,0:T(8,128)(2,1)} %bitcast.58, bf16[2048,2,128]{0,2,1:T(8,128)(2,1)} %bitcast.67), kind=kOutput, calls=%fused_computation.3 | convolution fusion | flops 2172645376 | bytes 39862272 | tf_op jit(solution)/shard_map/kqd,nkd->kqn/dot_general | solution.py:91
  70.4 0.0 copy-done.2
  70.4 15.2 %fusion.1 = f32[2,2048]{1,0:T(2,128)S(1)} fusion(f32[2,2048,2048]{1,2,0:T(8,128)} %get-tuple-element.11, f32[2,2048]{1,0:T(2,128)S(1)} %broadcast_maximum_fusion, pred[2048,2048]{0,1:T(8,128)(4,1)S(1)} %copy-done.2), kind=kLoop, calls=%fused_computation.4 | loop fusion | flops 41938944 | bytes 37781504 | tf_op jit(solution)/shard_map/reduce_sum | solution.py:103
  85.7 0.0 all-to-all-done
  85.7 3.2 %copy.69 = bf16[4,4,4,4,64,128]{5,4,3,2,0,1:T(8,128)(2,1)S(1)} copy(bf16[4,4,4,4,64,128]{5,4,3,2,1,0:T(8,128)(2,1)} %all-to-all-done) | data formatting | bytes 8388608 | tf_op jit(solution)/shard_map/all_to_all | solution.py:145
  88.8 2.9 %copy.70 = bf16[1,4,16,4,64,128]{5,4,3,1,0,2:T(8,128)(2,1)} copy(bf16[1,4,16,4,64,128]{5,4,3,2,1,0:T(8,128)(2,1)S(1)} %bitcast.52) | data formatting | bytes 8388608 | tf_op jit(solution)/shard_map/all_to_all | solution.py:145
  91.8 5.8 %all-to-all-start.1 = ((bf16[1,4,16,4,64,128]{5,4,3,1,0,2:T(8,128)(2,1)}), bf16[1,4,16,4,64,128]{5,4,3,1,0,2:T(8,128)(2,1)}, u32[]{:S(2)}, u32[]{:S(2)}) async-start(bf16[1,4,16,4,64,128]{5,4,3,1,0,2:T(8,128)(2,1)} %copy.70), calls=%async_computation.1 | async-start | bytes 8388608 | tf_op jit(solution)/shard_map/all_to_all | solution.py:144
  97.6 0.0 all-gather.5.cloned.1.call-done
  97.6 18.3 %divide_convert_fusion = bf16[2,2048,128]{2,1,0:T(8,128)(2,1)S(1)} fusion(bf16[2048,2,128]{0,2,1:T(8,128)(2,1)} %bitcast.68, f32[2,2048,2048]{1,2,0:T(8,128)} %get-tuple-element.11, f32[2,2048]{1,0:T(2,128)S(1)} %broadcast_maximum_fusion, pred[2048,2048]{0,1:T(8,128)(4,1)} %broadcast_compare_fusion, f32[2,2048]{1,0:T(2,128)S(1)} %fusion.1), kind=kOutput, calls=%fused_computation.12 | convolution fusion | flops 2190475264 | bytes 39878656 | tf_op jit(solution)/shard_map/kqn,nkd->kqd/dot_general | solution.py:104
  115.9 0.7 copy.67
  116.6 1.2 copy.83
  117.8 27.1 %all-to-all-done.1 = bf16[1,4,16,4,64,128]{5,4,3,1,0,2:T(8,128)(2,1)} async-done(((bf16[1,4,16,4,64,128]{5,4,3,1,0,2:T(8,128)(2,1)}), bf16[1,4,16,4,64,128]{5,4,3,1,0,2:T(8,128)(2,1)}, u32[]{:S(2)}, u32[]{:S(2)}) %all-to-all-start.1) | async-done | bytes 4194336 | tf_op jit(solution)/shard_map/all_to_all | solution.py:144
  144.9 3.1 %copy.71 = bf16[1,4,16,4,64,128]{5,4,3,2,1,0:T(8,128)(2,1)S(1)} copy(bf16[1,4,16,4,64,128]{5,4,3,1,0,2:T(8,128)(2,1)} %all-to-all-done.1) | data formatting | bytes 8388608 | tf_op jit(solution)/shard_map/all_to_all | solution.py:144
  148.1 0.0 copy-start.1
  148.1 3.0 %copy.72 = bf16[2,1,4,8,4,64,128]{6,5,4,3,2,0,1:T(8,128)(2,1)} copy(bf16[2,1,4,8,4,64,128]{6,5,4,3,0,2,1:T(8,128)(2,1)S(1)} %bitcast.53) | data formatting | bytes 8388608 | tf_op jit(solution)/shard_map/all_to_all | solution.py:144
  151.1 0.0 copy-done.1
  (10 shorter events, 0.1 us)
Async XLA Ops:
  7.2 21.5 %copy-start = (bf16[256,1024]{1,0:T(8,128)(2,1)S(1)}, bf16[256,1024]{1,0:T(8,128)(2,1)}, u32[]{:S(2)}) copy-start(bf16[256,1024]{1,0:T(8,128)(2,1)} %param.13) | copy-start | bytes 1572868
  7.2 46.3 %all-gather.3.cloned.1.call-start = ((), (), s32[]{:S(2)}) async-start(), calls=%async_computation.2 | async-start | bytes 1179648 | tf_op jit(solution)/shard_map/all_gather | solution.py:87
  23.4 7.1 %copy-start.3 = (bf16[256,2048]{1,0:T(8,128)(2,1)S(1)}, bf16[256,2048]{1,0:T(8,128)(2,1)}, u32[]{:S(2)}) copy-start(bf16[256,2048]{1,0:T(8,128)(2,1)} %param.11) | copy-start | bytes 3145732
  23.4 62.2 %all-to-all-start = ((bf16[4,4,4,4,64,128]{5,4,3,2,1,0:T(8,128)(2,1)}), bf16[4,4,4,4,64,128]{5,4,3,2,1,0:T(8,128)(2,1)}, u32[]{:S(2)}, u32[]{:S(2)}) async-start(bf16[4,4,4,4,64,128]{5,4,3,2,1,0:T(8,128)(2,1)} %bitcast.51), calls=%async_computation | async-start | bytes 8388608 | tf_op jit(solution)/shard_map/all_to_all | solution.py:145
  28.4 69.2 %all-gather.5.cloned.1.call-start = ((), (), s32[]{:S(2)}) async-start(), calls=%async_computation.3 | async-start | bytes 1179648 | tf_op jit(solution)/shard_map/all_gather | solution.py:88
  28.7 2.5 %copy-start.5 = (f32[2048]{0:T(1024)S(1)}, f32[2048]{0:T(1024)}, u32[]{:S(2)}) copy-start(f32[2048]{0:T(1024)} %param.14) | copy-start | bytes 24580
  31.4 1.4 copy-start.4
  53.5 16.9 %copy-start.2 = (pred[2048,2048]{0,1:T(8,128)(4,1)S(1)}, pred[2048,2048]{0,1:T(8,128)(4,1)}, u32[]{:S(2)}) copy-start(pred[2048,2048]{0,1:T(8,128)(4,1)} %broadcast_compare_fusion) | copy-start | bytes 12582916
  91.8 53.2 %all-to-all-start.1 = ((bf16[1,4,16,4,64,128]{5,4,3,1,0,2:T(8,128)(2,1)}), bf16[1,4,16,4,64,128]{5,4,3,1,0,2:T(8,128)(2,1)}, u32[]{:S(2)}, u32[]{:S(2)}) async-start(bf16[1,4,16,4,64,128]{5,4,3,1,0,2:T(8,128)(2,1)} %copy.70), calls=%async_computation.1 | async-start | bytes 8388608 | tf_op jit(solution)/shard_map/all_to_all | solution.py:144
  148.1 3.0 %copy-start.1 = (bf16[256,1024]{1,0:T(8,128)(2,1)S(1)}, bf16[256,1024]{1,0:T(8,128)(2,1)}, u32[]{:S(2)}) copy-start(bf16[256,1024]{1,0:T(8,128)(2,1)} %param.13) | copy-start | bytes 1572868
Sparse Core Ops, SparseCore 0:
  11.2 42.2 all-gather.2
  55.5 38.4 all-gather.4
where the time goes:
time: 159 us; the launch traced here: 158 us
  waiting for transfers between devices  42.3 us (27%)
  matrix products  36.4 us (23%)
  other arithmetic  30.7 us (19%)
  local copies, waits for them, and re-layouts  23.1 us (15%)
  between operations  14.4 us (9%)
  starting transfers between devices  11.1 us (7%)
    all_to_all x1, waiting for transfers between devices, shards(): lax.all_to_all(lax.all_to_all(outgoing, 'dec', split_axis=0, concat_axis=...  27.1 us
    dot_general x1, matrix products, shards(): jnp.einsum('kqn,nkd->kqd', weights.astype(jnp.bfloat16), piece_values.res...  18.3 us
    dot_general x1, matrix products, shards(): jnp.einsum('kqd,nkd->kqn', query_rows, piece_keys.reshape(count, kv_local...  16.9 us
    reduce_sum x1, other arithmetic, shards(): total = jnp.sum(weights, axis=2)  15.2 us
    all_gather x1, waiting for transfers between devices, shards(): piece_keys = lax.all_gather(keys_rot, ('pre', 'rep'), axis=0, tiled=True)  15.1 us
    all_to_all x2, local copies, waits for them, and re-layouts, shards(): lax.all_to_all(lax.all_to_all(outgoing, 'dec', split_axis=0, concat_axis=...  6.13 us
    all_to_all x2, local copies, waits for them, and re-layouts, shards(): lax.all_to_all(outgoing, 'dec', split_axis=0, concat_axis=2, tiled=True)  6.08 us
    all_to_all x1, starting transfers between devices, shards(): lax.all_to_all(lax.all_to_all(outgoing, 'dec', split_axis=0, concat_axis=...  5.82 us
  transfers between devices with their start and end apart: 4, of which 2 were waited for; matrix products, arithmetic and copies ran while one was open for 51% of the time, Pallas kernels for 0%

commit v1 on v0

--- a/solution.py
+++ b/solution.py
@@ -9,6 +9,29 @@
 BLOCK = 128
 rope_base = 1000000.0
 masked_score = -1e30
+
+
+def carry_the_widths(v0, mesh_ax):
+    local_part = lax.psum(1, mesh_ax)
+    tall = lax.axis_index(mesh_ax)
+    inter, r_now, carry = (local_part, tall, v0.shape[0])
+    all_blocks = tuple(((d, (d + 1) % inter) for d in range(inter)))
+    bank = tuple(((d, (d - 1) % inter) for d in range(inter)))
+    outcome_arr = jnp.zeros((*v0.shape[:0], inter * carry, *v0.shape[1:]), v0.dtype)
+    outcome_arr = lax.dynamic_update_slice_in_dim(outcome_arr, v0, r_now * carry, axis=0)
+    n_now = mixed_arr = v0
+    x_new = inter // 2
+    for w in range(1, x_new + 1):
+        n_now = lax.ppermute(n_now, axis_name=mesh_ax, perm=all_blocks)
+        outcome_arr = lax.dynamic_update_slice_in_dim(
+            outcome_arr, n_now, (r_now - w) % inter * carry, axis=0
+        )
+        if w < inter - x_new:
+            mixed_arr = lax.ppermute(mixed_arr, mesh_ax, bank)
+            outcome_arr = lax.dynamic_update_slice_in_dim(
+                outcome_arr, mixed_arr, (r_now + w) % inter * carry, axis=0
+            )
+    return outcome_arr
 
 
 def rotate(values, where_at):
@@ -84,7 +107,7 @@
     ).astype(jnp.bfloat16)
     local_values = values_biased.reshape(count, kv_local * HD)
     best = jnp.full((kv_local, per_group * row_count), masked_score, jnp.float32)
-    piece_keys = lax.all_gather(keys_rot, ("pre", "rep"), axis=0, tiled=True)
+    piece_keys = carry_the_widths(keys_rot, ("pre", "rep"))
     piece_values = lax.all_gather(local_values, ("pre", "rep"), axis=0, tiled=True)
     count = piece_keys.shape[0]
     scores = (

time: 159 us -> 176 us (1.11)
  starting transfers between devices: 11.1 us -> 24.6 us
  local copies, waits for them, and re-layouts: 23.1 us -> 31.6 us
  waiting for transfers between devices: 42.3 us -> 38.5 us
    all_gather x1 -> x0, waiting for transfers between devices: 15.1 us -> none  [shards(): piece_keys = lax.all_gather(keys_rot, ('pre', 'rep'), axis=0, tiled=True)]
    ppermute x0 -> x7, waiting for transfers between devices: none -> 15.1 us  [the longest x4 13.3 us: carry_the_widths(): n_now = lax.ppermute(n_now, axis_name=mesh_ax, perm=all_blocks)]
    ppermute x0 -> x7, starting transfers between devices: none -> 13.8 us  [the longest x3 10.7 us: carry_the_widths(): mixed_arr = lax.ppermute(mixed_arr, mesh_ax, bank)]
    dynamic_update_slice x0 -> x8, local copies, waits for them, and re-layouts: none -> 5.46 us  [the longest x4 2.71 us: carry_the_widths(): lax.dynamic_update_slice_in_dim(outcome_arr, n_now, (r_now - w) % inter *...]
    all_to_all x1, waiting for transfers between devices: 27.1 us -> 23.4 us  [shards(): lax.all_to_all(lax.all_to_all(outgoing, 'dec', split_axis=0, concat_axis=...]
    another operation x3, local copies, waits for them, and re-layouts: 0.63 us -> 2.57 us
    unnamed x18 -> x20, local copies, waits for them, and re-layouts: 4.5 us -> 4.5 us
  transfers between devices with their start and end apart: 4 -> 10, of which waited for: 2 -> 5; matrix products, arithmetic and copies ran while one was open for 51% -> 50% of each run, Pallas kernels for 0% -> 0%
where the time goes in v1:
time: 176 us; the launch traced here: 175 us
  waiting for transfers between devices  38.5 us (22%)
  matrix products  35.5 us (20%)
  local copies, waits for them, and re-layouts  31.6 us (18%)
  other arithmetic  30.2 us (17%)
  starting transfers between devices  24.6 us (14%)
  between operations  14.5 us (8%)
    all_to_all x1, waiting for transfers between devices, shards(): lax.all_to_all(lax.all_to_all(outgoing, 'dec', split_axis=0, concat_axis=...  23.4 us
    dot_general x1, matrix products, shards(): jnp.einsum('kqn,nkd->kqd', weights.astype(jnp.bfloat16), piece_values.res...  18.3 us
    dot_general x1, matrix products, shards(): jnp.einsum('kqd,nkd->kqn', query_rows, piece_keys.reshape(count, kv_local...  16 us
    reduce_sum x1, other arithmetic, shards(): total = jnp.sum(weights, axis=2)  15.1 us
    ppermute x4, waiting for transfers between devices, carry_the_widths(): n_now = lax.ppermute(n_now, axis_name=mesh_ax, perm=all_blocks)  13.3 us
    ppermute x3, starting transfers between devices, carry_the_widths(): mixed_arr = lax.ppermute(mixed_arr, mesh_ax, bank)  10.7 us
    all_to_all x2, local copies, waits for them, and re-layouts, shards(): lax.all_to_all(lax.all_to_all(outgoing, 'dec', split_axis=0, concat_axis=...  6.13 us
    all_to_all x2, local copies, waits for them, and re-layouts, shards(): lax.all_to_all(outgoing, 'dec', split_axis=0, concat_axis=2, tiled=True)  6.06 us
  transfers between devices with their start and end apart: 10, of which 5 were waited for; matrix products, arithmetic and copies ran while one was open for 50% of the time, Pallas kernels for 0%

profile of v1, /device:TPU:0, one launch (start us, length us, event | category | flops | bytes accessed | tf_op | source)
XLA Modules:
  0.0 174.9 jit_solution(4792872474891235849)
XLA Ops:
  7.2 0.0 copy-start
  7.2 0.0 all-gather.2.cloned.1.call-start
  7.3 1.1 dynamic-slice_convert_fusion
  8.4 0.1 copy.76
  8.5 0.8 dynamic-slice_bitcast_fusion
  9.3 0.1 broadcast_add_fusion
  9.4 0.8 fusion.14
  10.1 0.3 multiply_cosine_fusion
  10.5 3.1 %collective-permute-start = (bf16[256,256]{0,1:T(8,128)(2,1)S(1)}, bf16[256,256]{0,1:T(8,128)(2,1)S(1)}, u32[]{:S(2)}, u32[]{:S(2)}) collective-permute-start(bf16[256,256]{0,1:T(8,128)(2,1)S(1)} %bitcast.62), channel_id=1, source_target_pairs={{0,1},{1,2},{2,3},{3,16},{16,17},{17,18},{18,19},{19,0},{4,5},{5,6... | collective-permute-start | bytes 393224 | tf_op jit(solution)/shard_map/ppermute | solution.py:25
  13.6 3.0 %collective-permute-start.1 = (bf16[256,256]{0,1:T(8,128)(2,1)S(1)}, bf16[256,256]{0,1:T(8,128)(2,1)S(1)}, u32[]{:S(2)}, u32[]{:S(2)}) collective-permute-start(bf16[256,256]{0,1:T(8,128)(2,1)S(1)} %bitcast.63), channel_id=1, source_target_pairs={{0,19},{1,0},{2,1},{3,2},{16,3},{17,16},{18,17},{19,18},{4,23},{5,... | collective-permute-start | bytes 393224 | tf_op jit(solution)/shard_map/ppermute | solution.py:30
  16.7 0.1 copy.77
  16.8 0.8 dynamic_slice.24
  17.5 0.8 add_convert_fusion.1
  18.3 0.0 all-gather.2.cloned.1.call-update
  18.3 0.8 dynamic-slice_bitcast_fusion.1
  19.1 0.2 convert_reduce_fusion
  19.3 0.7 compare_select_fusion
  20.0 0.1 copy.68
  20.1 0.1 reduce-window.8
  20.1 0.1 reduce
  20.2 0.8 select_reduce_fusion
  21.1 0.1 fusion.8
  21.2 1.5 broadcast_multiply_fusion
  22.6 2.5 %mul.188 = bf16[8,131072]{1,0:T(8,128)(2,1)S(1)} reshape(bf16[1,8,4,4,64,128]{5,4,3,2,1,0:T(8,128)(2,1)} %broadcast_multiply_fusion) | data formatting | bytes 4194304 | tf_op jit(solution)/shard_map/mul | solution.py:151
  25.1 1.2 fusion.6
  26.4 2.7 %copy.81 = bf16[2,8,1024,128]{3,2,1,0:T(8,128)(2,1)} copy(bf16[2,8,1024,128]{3,1,2,0:T(8,128)(2,1)S(1)} %fusion.6) | data formatting | bytes 8388608
  29.1 5.0 %all-to-all-start = ((bf16[4,4,4,4,64,128]{5,4,3,2,1,0:T(8,128)(2,1)}), bf16[4,4,4,4,64,128]{5,4,3,2,1,0:T(8,128)(2,1)}, u32[]{:S(2)}, u32[]{:S(2)}) async-start(bf16[4,4,4,4,64,128]{5,4,3,2,1,0:T(8,128)(2,1)} %bitcast.51), calls=%async_computation | async-start | bytes 8388608 | tf_op jit(solution)/shard_map/all_to_all | solution.py:168
  34.2 0.1 copy.58
  34.3 0.1 copy.59
  34.4 1.1 broadcast_in_dim.26
  35.5 0.7 constant_dynamic-update-slice_fusion.7
  36.2 0.2 convert_bitcast_fusion
  36.5 0.4 copy.79
  36.9 0.1 bitcast_add_fusion
  37.0 0.8 subtract_convert_fusion
  37.8 1.2 copy.60
  39.0 1.2 copy.61
  40.3 4.1 %broadcast_compare_fusion = pred[2048,2048]{0,1:T(8,128)(4,1)} fusion(s32[2048]{0:T(1024)S(1)} %bitcast.65, s32[2048]{0:T(1024)S(1)} %copy-done.5), kind=kLoop, calls=%fused_computation.8 | loop fusion | flops 4194304 | bytes 4210688 | tf_op jit(solution)/shard_map/le | solution.py:122
  44.4 3.3 %pad_maximum_fusion = bf16[256,2,8,128]{3,0,2,1:T(8,128)(2,1)} fusion(bf16[256,2,8,64]{3,0,2,1:T(8,128)(2,1)} %bitcast.55, bf16[256,2,8,64]{3,0,2,1:T(8,128)(2,1)} %bitcast.54), kind=kLoop, calls=%fused_computation.16 | loop fusion | flops 2097152 | bytes 2097152 | tf_op jit(solution)/shard_map/concatenate | solution.py:46
  47.7 4.7 %collective-permute-start.3 = (bf16[256,256]{0,1:T(8,128)(2,1)S(1)}, bf16[256,256]{0,1:T(8,128)(2,1)S(1)}, u32[]{:S(2)}, u32[]{:S(2)}) collective-permute-start(bf16[256,256]{0,1:T(8,128)(2,1)S(1)} %collective-permute-done.1), channel_id=1, source_target_pairs={{0,19},{1,0},{2,1},{3,2},{16,3},{17,16},{18,17},{19,18},{4,23},{5,... | collective-permute-start | bytes 393224 | tf_op jit(solution)/shard_map/ppermute | solution.py:30
  52.4 0.7 constant_dynamic-update-slice_fusion.6
  53.1 0.7 constant_dynamic-update-slice_fusion.5
  53.8 4.5 %collective-permute-done.2 = bf16[256,256]{0,1:T(8,128)(2,1)S(1)} collective-permute-done((bf16[256,256]{0,1:T(8,128)(2,1)S(1)}, bf16[256,256]{0,1:T(8,128)(2,1)S(1)}, u32[]{:S(2)}, u32[]{:S(2)}) %collective-permute-start.2) | collective-permute-done | bytes 131104 | tf_op jit(solution)/shard_map/ppermute | solution.py:25
  58.2 1.8 %collective-permute-done.3 = bf16[256,256]{0,1:T(8,128)(2,1)S(1)} collective-permute-done((bf16[256,256]{0,1:T(8,128)(2,1)S(1)}, bf16[256,256]{0,1:T(8,128)(2,1)S(1)}, u32[]{:S(2)}, u32[]{:S(2)}) %collective-permute-start.3) | collective-permute-done | bytes 131104 | tf_op jit(solution)/shard_map/ppermute | solution.py:30
  60.0 2.9 %collective-permute-start.5 = (bf16[256,256]{0,1:T(8,128)(2,1)S(1)}, bf16[256,256]{0,1:T(8,128)(2,1)S(1)}, u32[]{:S(2)}, u32[]{:S(2)}) collective-permute-start(bf16[256,256]{0,1:T(8,128)(2,1)S(1)} %collective-permute-done.3), channel_id=1, source_target_pairs={{0,19},{1,0},{2,1},{3,2},{16,3},{17,16},{18,17},{19,18},{4,23},{5,... | collective-permute-start | bytes 393224 | tf_op jit(solution)/shard_map/ppermute | solution.py:30
  63.0 0.7 constant_dynamic-update-slice_fusion.4
  63.7 0.7 constant_dynamic-update-slice_fusion.3
  64.3 2.5 %collective-permute-done.4 = bf16[256,256]{0,1:T(8,128)(2,1)S(1)} collective-permute-done((bf16[256,256]{0,1:T(8,128)(2,1)S(1)}, bf16[256,256]{0,1:T(8,128)(2,1)S(1)}, u32[]{:S(2)}, u32[]{:S(2)}) %collective-permute-start.4) | collective-permute-done | bytes 131104 | tf_op jit(solution)/shard_map/ppermute | solution.py:25
  66.9 0.7 constant_dynamic-update-slice_fusion.2
  67.6 0.7 constant_dynamic-update-slice_fusion.1
  68.3 6.3 %collective-permute-done.6 = bf16[256,256]{0,1:T(8,128)(2,1)S(1)} collective-permute-done((bf16[256,256]{0,1:T(8,128)(2,1)S(1)}, bf16[256,256]{0,1:T(8,128)(2,1)S(1)}, u32[]{:S(2)}, u32[]{:S(2)}) %collective-permute-start.6) | collective-permute-done | bytes 131104 | tf_op jit(solution)/shard_map/ppermute | solution.py:25
  74.5 0.7 constant_dynamic-update-slice_fusion
  75.2 16.0 %fusion = (f32[2,2048]{1,0:T(2,128)S(1)}, f32[2,2048,2048]{1,2,0:T(8,128)}) fusion(pred[2048,2048]{0,1:T(8,128)(4,1)S(1)} %copy-done.2, bf16[2,2048,128]{2,1,0:T(8,128)(2,1)} %bitcast.58, bf16[2048,2,128]{0,2,1:T(8,128)(2,1)} %bitcast.8), kind=kOutput, calls=%fused_computation.3 | convolution fusion | flops 2172645376 | bytes 39862272 | tf_op jit(solution)/shard_map/kqd,nkd->kqn/dot_general | solution.py:114
  91.2 15.1 %fusion.1 = f32[2,2048]{1,0:T(2,128)S(1)} fusion(f32[2,2048,2048]{1,2,0:T(8,128)} %get-tuple-element.11, f32[2,2048]{1,0:T(2,128)S(1)} %broadcast_maximum_fusion, pred[2048,2048]{0,1:T(8,128)(4,1)S(1)} %copy-done.2), kind=kLoop, calls=%fused_computation.4 | loop fusion | flops 41938944 | bytes 37781504 | tf_op jit(solution)/shard_map/reduce_sum | solution.py:126
  106.3 3.1 %copy.69 = bf16[4,4,4,4,64,128]{5,4,3,2,0,1:T(8,128)(2,1)S(1)} copy(bf16[4,4,4,4,64,128]{5,4,3,2,1,0:T(8,128)(2,1)} %all-to-all-done) | data formatting | bytes 8388608 | tf_op jit(solution)/shard_map/all_to_all | solution.py:168
  109.5 2.9 %copy.70 = bf16[1,4,16,4,64,128]{5,4,3,1,0,2:T(8,128)(2,1)} copy(bf16[1,4,16,4,64,128]{5,4,3,2,1,0:T(8,128)(2,1)S(1)} %bitcast.52) | data formatting | bytes 8388608 | tf_op jit(solution)/shard_map/all_to_all | solution.py:168
  112.4 5.8 %all-to-all-start.1 = ((bf16[1,4,16,4,64,128]{5,4,3,1,0,2:T(8,128)(2,1)}), bf16[1,4,16,4,64,128]{5,4,3,1,0,2:T(8,128)(2,1)}, u32[]{:S(2)}, u32[]{:S(2)}) async-start(bf16[1,4,16,4,64,128]{5,4,3,1,0,2:T(8,128)(2,1)} %copy.70), calls=%async_computation.1 | async-start | bytes 8388608 | tf_op jit(solution)/shard_map/all_to_all | solution.py:167
  118.2 0.0 all-gather.2.cloned.1.call-done
  118.3 18.3 %divide_convert_fusion = bf16[2,2048,128]{2,1,0:T(8,128)(2,1)S(1)} fusion(f32[2,2048]{1,0:T(2,128)S(1)} %fusion.1, bf16[2048,2,128]{0,2,1:T(8,128)(2,1)} %bitcast.69, f32[2,2048,2048]{1,2,0:T(8,128)} %get-tuple-element.11, f32[2,2048]{1,0:T(2,128)S(1)} %broadcast_maximum_fusion, pred[2048,2048]{0,1:T(8,128)(4,1)} %broadcast_compare_fusion), kind=kOutput, calls=%fused_computation.12 | convolution fusion | flops 2190475264 | bytes 39878656 | tf_op jit(solution)/shard_map/kqn,nkd->kqd/dot_general | solution.py:127
  136.5 0.7 copy.67
  137.2 1.2 copy.83
  138.5 23.4 %all-to-all-done.1 = bf16[1,4,16,4,64,128]{5,4,3,1,0,2:T(8,128)(2,1)} async-done(((bf16[1,4,16,4,64,128]{5,4,3,1,0,2:T(8,128)(2,1)}), bf16[1,4,16,4,64,128]{5,4,3,1,0,2:T(8,128)(2,1)}, u32[]{:S(2)}, u32[]{:S(2)}) %all-to-all-start.1) | async-done | bytes 4194336 | tf_op jit(solution)/shard_map/all_to_all | solution.py:167
  161.9 3.1 %copy.71 = bf16[1,4,16,4,64,128]{5,4,3,2,1,0:T(8,128)(2,1)S(1)} copy(bf16[1,4,16,4,64,128]{5,4,3,1,0,2:T(8,128)(2,1)} %all-to-all-done.1) | data formatting | bytes 8388608 | tf_op jit(solution)/shard_map/all_to_all | solution.py:167
  165.1 3.0 %copy.72 = bf16[2,1,4,8,4,64,128]{6,5,4,3,2,0,1:T(8,128)(2,1)} copy(bf16[2,1,4,8,4,64,128]{6,5,4,3,0,2,1:T(8,128)(2,1)S(1)} %bitcast.53) | data formatting | bytes 8388608 | tf_op jit(solution)/shard_map/all_to_all | solution.py:167
  (31 shorter events, 0.2 us)
Async XLA Ops:
  7.2 9.5 %copy-start = (bf16[256,1024]{1,0:T(8,128)(2,1)S(1)}, bf16[256,1024]{1,0:T(8,128)(2,1)}, u32[]{:S(2)}) copy-start(bf16[256,1024]{1,0:T(8,128)(2,1)} %param.13) | copy-start | bytes 1572868
  7.2 14.0 %copy-start.3 = (bf16[1,8,4,4,64,128]{5,4,3,2,1,0:T(8,128)(2,1)S(1)}, bf16[1,8,4,4,64,128]{5,4,3,2,1,0:T(8,128)(2,1)}, u32[]{:S(2)}) copy-start(bf16[1,8,4,4,64,128]{5,4,3,2,1,0:T(8,128)(2,1)} %param.21) | copy-start | bytes 6291460
  7.2 111.1 %all-gather.2.cloned.1.call-start = ((), (), s32[]{:S(2)}) async-start(), calls=%async_computation.2 | async-start | bytes 1179648 | tf_op jit(solution)/shard_map/all_gather | solution.py:111
  10.5 37.2 %collective-permute-start = (bf16[256,256]{0,1:T(8,128)(2,1)S(1)}, bf16[256,256]{0,1:T(8,128)(2,1)S(1)}, u32[]{:S(2)}, u32[]{:S(2)}) collective-permute-start(bf16[256,256]{0,1:T(8,128)(2,1)S(1)} %bitcast.62), channel_id=1, source_target_pairs={{0,1},{1,2},{2,3},{3,16},{16,17},{17,18},{18,19},{19,0},{4,5},{5,6... | collective-permute-start | bytes 393224 | tf_op jit(solution)/shard_map/ppermute | solution.py:25
  13.6 34.1 %collective-permute-start.1 = (bf16[256,256]{0,1:T(8,128)(2,1)S(1)}, bf16[256,256]{0,1:T(8,128)(2,1)S(1)}, u32[]{:S(2)}, u32[]{:S(2)}) collective-permute-start(bf16[256,256]{0,1:T(8,128)(2,1)S(1)} %bitcast.63), channel_id=1, source_target_pairs={{0,19},{1,0},{2,1},{3,2},{16,3},{17,16},{18,17},{19,18},{4,23},{5,... | collective-permute-start | bytes 393224 | tf_op jit(solution)/shard_map/ppermute | solution.py:30
  29.1 7.1 %copy-start.4 = (bf16[256,2048]{1,0:T(8,128)(2,1)S(1)}, bf16[256,2048]{1,0:T(8,128)(2,1)}, u32[]{:S(2)}) copy-start(bf16[256,2048]{1,0:T(8,128)(2,1)} %param.11) | copy-start | bytes 3145732
  29.1 77.2 %all-to-all-start = ((bf16[4,4,4,4,64,128]{5,4,3,2,1,0:T(8,128)(2,1)}), bf16[4,4,4,4,64,128]{5,4,3,2,1,0:T(8,128)(2,1)}, u32[]{:S(2)}, u32[]{:S(2)}) async-start(bf16[4,4,4,4,64,128]{5,4,3,2,1,0:T(8,128)(2,1)} %bitcast.51), calls=%async_computation | async-start | bytes 8388608 | tf_op jit(solution)/shard_map/all_to_all | solution.py:168
  34.4 2.4 %copy-start.6 = (f32[2048]{0:T(1024)S(1)}, f32[2048]{0:T(1024)}, u32[]{:S(2)}) copy-start(f32[2048]{0:T(1024)} %param.14) | copy-start | bytes 24580
  37.0 3.3 %copy-start.5 = (s32[2048]{0:T(1024)S(1)}, s32[2048]{0:T(1024)}, u32[]{:S(2)}) copy-start(s32[2048]{0:T(1024)} %param.17) | copy-start | bytes 24580
  44.4 30.8 %copy-start.2 = (pred[2048,2048]{0,1:T(8,128)(4,1)S(1)}, pred[2048,2048]{0,1:T(8,128)(4,1)}, u32[]{:S(2)}) copy-start(pred[2048,2048]{0,1:T(8,128)(4,1)} %broadcast_compare_fusion) | copy-start | bytes 12582916
  47.7 10.5 %collective-permute-start.2 = (bf16[256,256]{0,1:T(8,128)(2,1)S(1)}, bf16[256,256]{0,1:T(8,128)(2,1)S(1)}, u32[]{:S(2)}, u32[]{:S(2)}) collective-permute-start(bf16[256,256]{0,1:T(8,128)(2,1)S(1)} %collective-permute-done), channel_id=1, source_target_pairs={{0,1},{1,2},{2,3},{3,16},{16,17},{17,18},{18,19},{19,0},{4,5},{5,6... | collective-permute-start | bytes 393224 | tf_op jit(solution)/shard_map/ppermute | solution.py:25
  47.7 12.3 %collective-permute-start.3 = (bf16[256,256]{0,1:T(8,128)(2,1)S(1)}, bf16[256,256]{0,1:T(8,128)(2,1)S(1)}, u32[]{:S(2)}, u32[]{:S(2)}) collective-permute-start(bf16[256,256]{0,1:T(8,128)(2,1)S(1)} %collective-permute-done.1), channel_id=1, source_target_pairs={{0,19},{1,0},{2,1},{3,2},{16,3},{17,16},{18,17},{19,18},{4,23},{5,... | collective-permute-start | bytes 393224 | tf_op jit(solution)/shard_map/ppermute | solution.py:30
  58.2 8.6 %collective-permute-start.4 = (bf16[256,256]{0,1:T(8,128)(2,1)S(1)}, bf16[256,256]{0,1:T(8,128)(2,1)S(1)}, u32[]{:S(2)}, u32[]{:S(2)}) collective-permute-start(bf16[256,256]{0,1:T(8,128)(2,1)S(1)} %collective-permute-done.2), channel_id=1, source_target_pairs={{0,1},{1,2},{2,3},{3,16},{16,17},{17,18},{18,19},{19,0},{4,5},{5,6... | collective-permute-start | bytes 393224 | tf_op jit(solution)/shard_map/ppermute | solution.py:25
  60.0 7.5 %collective-permute-start.5 = (bf16[256,256]{0,1:T(8,128)(2,1)S(1)}, bf16[256,256]{0,1:T(8,128)(2,1)S(1)}, u32[]{:S(2)}, u32[]{:S(2)}) collective-permute-start(bf16[256,256]{0,1:T(8,128)(2,1)S(1)} %collective-permute-done.3), channel_id=1, source_target_pairs={{0,19},{1,0},{2,1},{3,2},{16,3},{17,16},{18,17},{19,18},{4,23},{5,... | collective-permute-start | bytes 393224 | tf_op jit(solution)/shard_map/ppermute | solution.py:30
  66.9 7.7 %collective-permute-start.6 = (bf16[256,256]{0,1:T(8,128)(2,1)S(1)}, bf16[256,256]{0,1:T(8,128)(2,1)S(1)}, u32[]{:S(2)}, u32[]{:S(2)}) collective-permute-start(bf16[256,256]{0,1:T(8,128)(2,1)S(1)} %collective-permute-done.4), channel_id=1, source_target_pairs={{0,1},{1,2},{2,3},{3,16},{16,17},{17,18},{18,19},{19,0},{4,5},{5,6... | collective-permute-start | bytes 393224 | tf_op jit(solution)/shard_map/ppermute | solution.py:25
  112.4 49.5 %all-to-all-start.1 = ((bf16[1,4,16,4,64,128]{5,4,3,1,0,2:T(8,128)(2,1)}), bf16[1,4,16,4,64,128]{5,4,3,1,0,2:T(8,128)(2,1)}, u32[]{:S(2)}, u32[]{:S(2)}) async-start(bf16[1,4,16,4,64,128]{5,4,3,1,0,2:T(8,128)(2,1)} %copy.70), calls=%async_computation.1 | async-start | bytes 8388608 | tf_op jit(solution)/shard_map/all_to_all | solution.py:167
  165.0 3.0 %copy-start.1 = (bf16[256,1024]{1,0:T(8,128)(2,1)S(1)}, bf16[256,1024]{1,0:T(8,128)(2,1)}, u32[]{:S(2)}) copy-start(bf16[256,1024]{1,0:T(8,128)(2,1)} %param.13) | copy-start | bytes 1572868
Sparse Core Ops, SparseCore 0:
  18.4 42.7 all-gather.1
